TPU v7x, 32 devices: a whole 2x2x4 slice. The times are simulated.
32 devices in a mesh: tile: 8 (over z, x), slab: 4 (over y, core).
Axes of the slice: x: 2, y: 2, z: 4, core: 2. Of those that a mesh axis runs over, the one named last changes fastest.
Arguments:
- object_field: bfloat16 [2, 8, 1024, 512], P(None, 'slab', 'tile')
- probe_wave: bfloat16 [2, 128, 128], replicated, may hold values from -6 to 6
- prop_phase: float32 [128, 128], replicated, may hold values from -3.140625 to 3.140625
- intensity: float32 [16, 128, 128], P('tile'), may hold values from 0 to 4
- patch_rows: int32 [16], replicated, may hold values from 0 to 127
- patch_cols: int32 [16], replicated, may hold values from 0 to 384
Outputs:
- grad_object: bfloat16 [2, 8, 1024, 512], P(None, 'slab', 'tile')
Inputs may be any that keep to these rules, and one draw needn't show every extreme that they name: `patch_rows`: a window of tile t covers rows of tile t and of the next tile (the first tile after the last).
All inputs are finite; a program needn't handle non-finite values.
Results may differ from a plain program's by a relative error of at most 0.005.
Values may be sent and summed in bfloat16 or wider, within the bound.
A program may use at most 64 MiB of HBM per device.

v0:
```python
import math

import jax
import jax.numpy as jnp
from jax import lax
from jax.sharding import PartitionSpec as P


def from_behind(value, axis, by):
    peers = lax.axis_size(axis)
    return lax.ppermute(value, axis, [(i, (i + by) % peers) for i in range(peers)])


def partner(block, axis, stride):
    count = lax.axis_size(axis)
    route = []
    for low in range(count):
        high = low | 1 << stride
        if high != low and high < count:
            route += [(low, high), (high, low)]
    return lax.ppermute(block, axis, route)


def from_behind_2(value, axis, by):
    peers = lax.axis_size(axis)
    pairs = [(i, i + by) for i in range(peers) if 0 <= i + by < peers]
    return lax.ppermute(value, axis, pairs)


def fourier_tables(window, exponent_sign):
    indices = jnp.arange(window, dtype=jnp.int32)
    product = indices[:, None] * indices[None, :] % window
    angles = product.astype(jnp.float32) * (exponent_sign * 2.0 * math.pi / window)
    scaling = 1.0 / math.sqrt(window)
    real_part = jnp.cos(angles) * scaling
    imag_part = jnp.sin(angles) * scaling
    left_table = jnp.concatenate([real_part, imag_part], axis=0)
    right_table = jnp.concatenate(
        [
            jnp.concatenate([real_part, imag_part], axis=1),
            jnp.concatenate([-imag_part, real_part], axis=1),
        ],
        axis=0,
    )
    return (left_table, right_table)


def transform_all(field_in, tables, window):
    left_table, right_table = tables
    batch_size = field_in.shape[0]
    flat = field_in.reshape(batch_size * window, 2 * window)
    first_pass = jnp.dot(
        flat, right_table, precision=lax.Precision.HIGHEST, preferred_element_type=jnp.float32
    )
    first_pass = first_pass.reshape(batch_size, window, 2 * window)
    second_pass = jnp.einsum(
        "ka,pab->pkb",
        left_table,
        first_pass,
        precision=lax.Precision.HIGHEST,
        preferred_element_type=jnp.float32,
    )
    upper_half = second_pass[:, :window]
    lower_half = second_pass[:, window:]
    return jnp.concatenate(
        [
            upper_half[..., :window] - lower_half[..., window:],
            upper_half[..., window:] + lower_half[..., :window],
        ],
        axis=-1,
    )


def complex_times(left_side, right_side, window):
    left_re = left_side[..., :window]
    left_im = left_side[..., window:]
    right_re = right_side[..., :window].astype(jnp.float32)
    right_im = right_side[..., window:].astype(jnp.float32)
    return jnp.concatenate(
        [left_re * right_re - left_im * right_im, left_re * right_im + left_im * right_re], axis=-1
    )


def conj_times(left_side, right_side, window):
    left_re = left_side[..., :window].astype(jnp.float32)
    left_im = left_side[..., window:].astype(jnp.float32)
    right_re = right_side[..., :window]
    right_im = right_side[..., window:]
    return jnp.concatenate(
        [left_re * right_re + left_im * right_im, left_re * right_im - left_im * right_re], axis=-1
    )


def cut_blocks(object_field, column_list, window):

    def cut_one(column):
        block_piece = lax.dynamic_slice_in_dim(object_field, column, window, axis=3)
        return jnp.concatenate([block_piece[0], block_piece[1]], axis=2)

    return jax.vmap(cut_one, out_axes=1)(column_list)


def add_block(gradient, block, column, window, layers):
    zero_index = jnp.zeros((), jnp.int32)
    paired = jnp.stack([block[..., :window], block[..., window:]])
    where_at = (zero_index, zero_index, zero_index, column)
    current = lax.dynamic_slice(gradient, where_at, (2, layers, window, window))
    return lax.dynamic_update_slice(gradient, current + paired, where_at)


def body(object_field, probe_wave, prop_phase, intensity, patch_rows, patch_cols):
    window = probe_wave.shape[1]
    layers = object_field.shape[1]
    columns = object_field.shape[3]
    per_tile = intensity.shape[0]
    tile_count = lax.axis_size("tile")
    section_count = lax.axis_size("slab")
    tile_here = lax.axis_index("tile")
    section_here = lax.axis_index("slab")
    tile_before = (tile_here + tile_count - 1) % tile_count
    own_rows = lax.dynamic_slice_in_dim(patch_rows, tile_here * per_tile, per_tile)
    own_cols = lax.dynamic_slice_in_dim(patch_cols, tile_here * per_tile, per_tile)
    prior_cols = lax.dynamic_slice_in_dim(patch_cols, tile_before * per_tile, per_tile)
    forward_tables = fourier_tables(window, -1.0)
    backward_tables = fourier_tables(window, 1.0)
    propagator = jnp.concatenate([jnp.cos(prop_phase), jnp.sin(prop_phase)], axis=1)
    probe_batch = jnp.concatenate([probe_wave[0], probe_wave[1]], axis=1)[None].astype(jnp.float32)
    cut_sent = cut_blocks(object_field, prior_cols, window)
    arrived = from_behind(cut_sent, "tile", -1)
    own_blocks = cut_blocks(object_field, own_cols, window)
    stacked = jnp.concatenate([own_blocks, arrived], axis=2)

    def pick_rows(block_pair, row_start):
        return lax.dynamic_slice_in_dim(block_pair, row_start, window, axis=1)

    patches = jax.vmap(pick_rows, in_axes=(1, 0), out_axes=1)(stacked, own_rows)

    def propagate(field_in):
        moved = complex_times(propagator, transform_all(field_in, forward_tables, window), window)
        return transform_all(moved, backward_tables, window)

    def back_propagate(field_in):
        returned = conj_times(propagator, transform_all(field_in, forward_tables, window), window)
        return transform_all(returned, backward_tables, window)

    def forward_section(incoming, patch_set, measured, last_flag):
        section_layers = patch_set.shape[0]
        stored = []
        outgoing = incoming
        for layer_index in range(section_layers):
            stored.append(incoming)
            outgoing = complex_times(incoming, patch_set[layer_index], window)
            if layer_index < section_layers - 1:
                incoming = propagate(outgoing)

        def far_gradient(field_in):
            far_field = transform_all(field_in, forward_tables, window)
            far_power = far_field[..., :window] ** 2 + far_field[..., window:] ** 2
            misfit = far_power - measured
            far_grad = jnp.concatenate([misfit, misfit], axis=-1) * far_field
            return transform_all(far_grad, backward_tables, window)

        result = lax.cond(last_flag, far_gradient, propagate, outgoing)
        return (jnp.stack(stored), result)

    def backward_section(out_grad, stored, patch_set, first_flag):
        section_layers = patch_set.shape[0]
        grad_terms = [None] * section_layers
        for layer_index in reversed(range(section_layers)):
            grad_terms[layer_index] = conj_times(stored[layer_index], out_grad, window)
            in_grad = conj_times(patch_set[layer_index], out_grad, window)
            if layer_index > 0:
                out_grad = back_propagate(in_grad)
            else:
                out_grad = lax.cond(first_flag, jnp.zeros_like, back_propagate, in_grad)
        return (jnp.stack(grad_terms), out_grad)

    def keep_same(inner):
        return inner

    half_count = per_tile // 2
    parity = section_here % 2
    is_lower = parity == 0
    group_here = section_here // 2
    group_count = section_count // 2
    partner_start = (1 - parity) * half_count
    mine_start = parity * half_count
    sent_patches = lax.dynamic_slice_in_dim(patches, partner_start, half_count, axis=1)
    partner_patches = partner(sent_patches, "slab", 0)
    mine_patches = lax.dynamic_slice_in_dim(patches, mine_start, half_count, axis=1)
    joined = jnp.where(
        is_lower,
        jnp.concatenate([mine_patches, partner_patches], axis=0),
        jnp.concatenate([partner_patches, mine_patches], axis=0),
    )
    measured_half = lax.dynamic_slice_in_dim(intensity, mine_start, half_count, axis=0)
    pair_last = group_here == group_count - 1
    pair_first = group_here == 0
    half_shape = (half_count, window, 2 * window)
    pair_stored = jnp.zeros((2 * layers,) + half_shape, jnp.float32)
    pair_grads = jnp.zeros((2 * layers,) + half_shape, jnp.float32)
    wave_now = jnp.zeros(half_shape, jnp.float32)

    def pair_forward(turn_index, carried):
        stored_now, wave_in = carried
        wave_in = from_behind_2(wave_in, "slab", 2)

        def run_group(inner):
            incoming = jnp.where(pair_first, probe_batch, inner[1])
            return forward_section(incoming, joined, measured_half, pair_last)

        return lax.cond(group_here == turn_index, run_group, keep_same, (stored_now, wave_in))

    pair_stored, wave_now = lax.fori_loop(0, group_count, pair_forward, (pair_stored, wave_now))
    pair_start = wave_now

    def pair_backward(turn_index, carried):
        grads_now, wave_in = carried
        wave_in = from_behind_2(wave_in, "slab", -2)

        def run_group(inner):
            out_grad = jnp.where(pair_last, pair_start, inner[1])
            return backward_section(out_grad, pair_stored, joined, pair_first)

        return lax.cond(
            group_here == group_count - 1 - turn_index, run_group, keep_same, (grads_now, wave_in)
        )

    pair_grads, wave_now = lax.fori_loop(0, group_count, pair_backward, (pair_grads, wave_now))
    lower_grads = pair_grads[:layers]
    upper_grads = pair_grads[layers:]
    mine_grads = jnp.where(is_lower, lower_grads, upper_grads)
    partner_grads = jnp.where(is_lower, upper_grads, lower_grads)
    returned_grads = partner(partner_grads.astype(jnp.bfloat16), "slab", 0).astype(
        partner_grads.dtype
    )
    grad_terms = jnp.where(
        is_lower,
        jnp.concatenate([mine_grads, returned_grads], axis=1),
        jnp.concatenate([returned_grads, mine_grads], axis=1),
    )

    def place_one(term_block, row_start):
        zero_index = jnp.zeros((), jnp.int32)
        placed = jnp.zeros((layers, 2 * window, 2 * window), jnp.float32)
        return lax.dynamic_update_slice(placed, term_block, (zero_index, row_start, zero_index))

    placed_all = jax.vmap(place_one, in_axes=(1, 0), out_axes=1)(grad_terms, own_rows)
    spilled = placed_all[:, :, window:]
    received = from_behind(spilled, "tile", 1)
    gradient = jnp.zeros((2, layers, window, columns), jnp.float32)
    for member in range(per_tile):
        gradient = add_block(
            gradient, placed_all[:, member, :window], own_cols[member], window, layers
        )
        gradient = add_block(gradient, received[:, member], prior_cols[member], window, layers)
    return gradient.astype(jnp.bfloat16)


def solution(mesh):
    return jax.shard_map(
        body,
        mesh=mesh,
        in_specs=(P(None, "slab", "tile", None), P(), P(), P("tile", None, None), P(), P()),
        out_specs=P(None, "slab", "tile", None),
        check_vma=False,
    )
```

profile of v0, /device:TPU:0, one launch (start us, length us, event | category | flops | bytes accessed | tf_op | source)
XLA Modules:
  0.0 122.3 jit_solution(13186868224014698546)
XLA Ops:
  0.0 1.4 %copy.30 = bf16[2,2,128,512]{2,1,0,3:T(2,128)(2,1)S(1)} copy(bf16[2,2,128,512]{3,2,1,0:T(8,128)(2,1)} %param.18) | data formatting | bytes 1048576 | tf_op args[0]
  1.5 1.1 gather_fusion.1
  3.1 6.1 %collective-permute-start.2 = (bf16[2,2,128,256]{2,0,3,1:T(2,128)(2,1)S(1)}, bf16[2,2,128,256]{2,0,3,1:T(2,128)(2,1)S(1)}, u32[]{:S(2)}, u32[]{:S(2)}) collective-permute-start(bf16[2,2,128,256]{2,0,3,1:T(2,128)(2,1)S(1)} %maximum_bitcast_fusion.37), channel_id=1, source_target_pairs={{0,28},{4,0},{8,4},{12,8},{16,12},{20,16},{24,20},{28,24},{1,29},{... | collective-permute-start | bytes 786440 | tf_op jit(solution)/shard_map/ppermute | solution.py:11
  10.2 1.1 gather_fusion
  15.9 1.3 %copy.35 = bf16[2,2,256,256]{3,1,0,2:T(2,128)(2,1)S(1)} copy(bf16[2,2,256,256]{2,1,3,0:T(2,128)(2,1)S(1)} %maximum_bitcast_fusion.35) | data formatting | bytes 1048576 | tf_op jit(solution)/shard_map/vmap()/transpose | solution.py:134
  17.2 1.2 gather_fusion.2
  27.0 19.6 %while.31 = (s32[]{:T(128)}, f32[4,1,128,256]{2,3,1,0:T(8,128)S(1)}, f32[1,128,256]{1,2,0:T(8,128)S(1)}, s32[]{:T(128)}, pred[]{:T(512)}, /*index=5*/f32[1,128,2...) while((s32[]{:T(128)}, ...), condition=%wide.region_5.6_spmd, body=%wide.region_0.5_spmd.sunk | while | flops 1612742656 | bytes 18743808 | solution.py:214
  27.0 3.4 %collective-permute-start = (f32[1,128,256]{1,2,0:T(8,128)S(1)}, f32[1,128,256]{1,2,0:T(8,128)S(1)}, u32[]{:S(2)}, u32[]{:S(2)}) collective-permute-start(f32[1,128,256]{1,2,0:T(8,128)S(1)} %get-tuple-element.1180), channel_id=1, source_target_pairs={{0,2},{1,3},{4,6},{5,7},{8,10},{9,11},{12,14},{13,15},{16,18},{17,... | collective-permute-start | bytes 393224 | tf_op jit(solution)/shard_map/while/body/eval_jaxpr/ppermute | solution.py:27
  30.4 3.4 %collective-permute-done = f32[1,128,256]{1,2,0:T(8,128)S(1)} collective-permute-done((f32[1,128,256]{1,2,0:T(8,128)S(1)}, f32[1,128,256]{1,2,0:T(8,128)S(1)}, u32[]{:S(2)}, u32[]{:S(2)}) %collective-permute-start) | collective-permute-done | bytes 131104 | tf_op jit(solution)/shard_map/while/body/eval_jaxpr/ppermute | solution.py:27
  33.8 8.6 %conditional.6 = ((f32[4,1,128,256]{2,3,1,0:T(8,128)S(1)}, f32[1,128,256]{1,2,0:T(8,128)S(1)})) conditional(s32[]{:T(128)} %convert_element_type.232, (f32[4,1,128,256]{2,3,1,0:T(8,128)S(1)}, f32[1,128,256]{1,2,0:T(8,128)S(1)}) %tuple.174, (pred[]{:T(512)}, f32[1,128,256]{1,2,0:T(8,128)S(1)}, f32[1,128,256]{1,2,0:T(8,128)S(1)}, ...), branch_computations={%region_1.1_spmd, %region_2.4_spmd} | conditional | flops 1612742656 | bytes 17957062 | solution.py:212
  39.1 1.7 %conditional = (f32[1,128,256]{1,2,0:T(8,128)S(1)}) conditional(s32[]{:T(128)} %convert_element_type.84, (f32[128,128]{0,1:T(8,128)S(1)}, f32[1,128,256]{1,2,0:T(8,128)S(1)}, f32[256,256]{1,0:T(8,128)S(1)}, f32[256,128]{1,0:T(8,128)S(1)}, f32[128,128]{0,1:T(8,128)S(1)}, /*index=5*/f32[256,256]{1,0:T(8,128)S(1)}, f32[256,128]{1,0:T(8,128)S(1)}) %tuple.45, ...), branch_computations={%region_3.2_spmd, %region_4.3_spmd} | conditional | flops 402915328 | bytes 3342344 | solution.py:163
  42.5 1.3 %collective-permute-start = (f32[1,128,256]{1,2,0:T(8,128)S(1)}, f32[1,128,256]{1,2,0:T(8,128)S(1)}, u32[]{:S(2)}, u32[]{:S(2)}) collective-permute-start(f32[1,128,256]{1,2,0:T(8,128)S(1)} %get-tuple-element.1180), channel_id=1, source_target_pairs={{0,2},{1,3},{4,6},{5,7},{8,10},{9,11},{12,14},{13,15},{16,18},{17,... | collective-permute-start | bytes 393224 | tf_op jit(solution)/shard_map/while/body/eval_jaxpr/ppermute | solution.py:27
  43.8 2.8 %collective-permute-done = f32[1,128,256]{1,2,0:T(8,128)S(1)} collective-permute-done((f32[1,128,256]{1,2,0:T(8,128)S(1)}, f32[1,128,256]{1,2,0:T(8,128)S(1)}, u32[]{:S(2)}, u32[]{:S(2)}) %collective-permute-start) | collective-permute-done | bytes 131104 | tf_op jit(solution)/shard_map/while/body/eval_jaxpr/ppermute | solution.py:27
  46.7 35.2 %while.32 = (s32[]{:T(128)}, f32[4,1,128,256]{2,3,1,0:T(8,128)S(1)}, f32[1,128,256]{1,2,0:T(8,128)S(1)}, s32[]{:T(128)}, f32[4,1,128,256]{2,3,1,0:T(8,128)S(1)},...) while((s32[]{:T(128)}, ...), condition=%wide.region_11.12_spmd, body=%wide.region_6.11_spmd.sunk | while | flops 1613135872 | bytes 21037532 | solution.py:229
  46.9 1.3 %collective-permute-start.1 = (f32[1,128,256]{1,2,0:T(8,128)S(1)}, f32[1,128,256]{1,2,0:T(8,128)S(1)}, u32[]{:S(2)}, u32[]{:S(2)}) collective-permute-start(f32[1,128,256]{1,2,0:T(8,128)S(1)} %get-tuple-element.1228), channel_id=1, source_target_pairs={{2,0},{3,1},{6,4},{7,5},{10,8},{11,9},{14,12},{15,13},{18,16},{19,... | collective-permute-start | bytes 393224 | tf_op jit(solution)/shard_map/while/body/eval_jaxpr/ppermute | solution.py:27
  48.2 14.0 %collective-permute-done.1 = f32[1,128,256]{1,2,0:T(8,128)S(1)} collective-permute-done((f32[1,128,256]{1,2,0:T(8,128)S(1)}, f32[1,128,256]{1,2,0:T(8,128)S(1)}, u32[]{:S(2)}, u32[]{:S(2)}) %collective-permute-start.1) | collective-permute-done | bytes 131104 | tf_op jit(solution)/shard_map/while/body/eval_jaxpr/ppermute | solution.py:27
  62.3 1.3 %collective-permute-start.1 = (f32[1,128,256]{1,2,0:T(8,128)S(1)}, f32[1,128,256]{1,2,0:T(8,128)S(1)}, u32[]{:S(2)}, u32[]{:S(2)}) collective-permute-start(f32[1,128,256]{1,2,0:T(8,128)S(1)} %get-tuple-element.1228), channel_id=1, source_target_pairs={{2,0},{3,1},{6,4},{7,5},{10,8},{11,9},{14,12},{15,13},{18,16},{19,... | collective-permute-start | bytes 393224 | tf_op jit(solution)/shard_map/while/body/eval_jaxpr/ppermute | solution.py:27
  63.6 11.2 %collective-permute-done.1 = f32[1,128,256]{1,2,0:T(8,128)S(1)} collective-permute-done((f32[1,128,256]{1,2,0:T(8,128)S(1)}, f32[1,128,256]{1,2,0:T(8,128)S(1)}, u32[]{:S(2)}, u32[]{:S(2)}) %collective-permute-start.1) | collective-permute-done | bytes 131104 | tf_op jit(solution)/shard_map/while/body/eval_jaxpr/ppermute | solution.py:27
  74.8 7.0 %conditional.7 = ((f32[4,1,128,256]{2,3,1,0:T(8,128)S(1)}, f32[1,128,256]{1,2,0:T(8,128)S(1)})) conditional(s32[]{:T(128)} %convert_element_type.233, (f32[4,1,128,256]{2,3,1,0:T(8,128)S(1)}, f32[1,128,256]{1,2,0:T(8,128)S(1)}) %tuple.177, (f32[4,1,128,256]{2,3,1,0:T(8,128)S(1)}, f32[128,128]{0,1:T(8,128)S(1)}, ...), branch_computations={%region_7.7_spmd, %region_8.10_spmd} | conditional | flops 1613135872 | bytes 20250774 | solution.py:225
  82.2 1.3 %collective-permute-done.4 = bf16[2,1,128,256]{3,2,0,1:T(8,128)(2,1)S(1)} collective-permute-done((bf16[2,1,128,256]{3,2,0,1:T(8,128)(2,1)S(1)}, bf16[2,1,128,256]{3,2,0,1:T(8,128)(2,1)S(1)}, u32[]{:S(2)}, u32[]{:S(2)}) %collective-permute-start.4) | collective-permute-done | bytes 131104 | tf_op jit(solution)/shard_map/ppermute | solution.py:21
  84.2 16.0 %while.33 = (s32[]{:T(128)}, f32[2,2,256,256]{3,2,1,0:T(8,128)S(1)}, s32[2,4]{1,0:T(2,128)S(1)}, f32[2,2,128,256]{3,2,1,0:T(8,128)S(1)}, s32[]{:T(128)}, /*index=5*/s32[4]{0:T(128)S(1)}, s32[]{:T(128)}) while((s32[]{:T(128)}, f32[2,2,256,256]{3,2,1,0:T(8,128)S(1)}, s32[2,4]{1,0:T(2,128)S(1)}, f32[2,2,128,256]{3,2,1,0:T(8,128)S(1)}, s32[]{:T(128)}, ...), condition=%wide.while_cond, body=%wide.while_body.sunk | while | flops 65565 | bytes 1310915 | solution.py:246
  84.9 3.3 %and_reduce_fusion.2 = pred[]{:T(512)} fusion(s32[4]{0:T(128)S(1)} %get-tuple-element.1277, s32[1]{0:T(128)} %bitcast.405, s32[1]{0:T(128)} %bitcast.406, s32[1]{0:T(128)} %bitcast.407, s32[1]{0:T(128)} %bitcast.408), kind=kLoop, calls=%fused_computation.277.clone.1 | loop fusion | flops 27 | bytes 33 | tf_op jit(solution)/shard_map/vmap(vmap())/scatter
  88.1 2.0 %dynamic-slice_select_fusion.2 = f32[1,2,128,256]{3,2,1,0:T(8,128)S(1)} fusion(f32[2,2,128,256]{3,2,1,0:T(8,128)S(1)} %get-tuple-element.1275, s32[]{:T(128)} %get-tuple-element.1265, f32[2,2,256,256]{3,2,1,0:T(8,128)S(1)} %get-tuple-element.1266, s32[]{:T(128)} %bitcast.403, s32[]{:T(128)} %bitcast.404, pred[]{:T(512)} %and_reduce_fusion.2), kind=kLoop, calls=%fused_computation.276.clone.1 | loop fusion | flops 65536 | bytes 786445 | tf_op jit(solution)/shard_map/vmap(vmap())/scatter
  90.1 2.0 %dynamic-update-slice.3 = f32[2,2,256,256]{3,2,1,0:T(8,128)S(1)} dynamic-update-slice(f32[2,2,256,256]{3,2,1,0:T(8,128)S(1)} %get-tuple-element.1266, f32[1,2,128,256]{3,2,1,0:T(8,128)S(1)} %dynamic-slice_select_fusion.2, s32[]{:T(128)} %bitcast.403, s32[]{:T(128)} %constant.93.clone.1..sunk, s32[]{:T(128)} %bitcast.404, s32[]{:T(128)} %constant.93.clone.1..sunk) | dynamic-update-slice | bytes 524292 | tf_op jit(solution)/shard_map/vmap(vmap())/scatter
  92.8 3.3 %and_reduce_fusion.2 = pred[]{:T(512)} fusion(s32[4]{0:T(128)S(1)} %get-tuple-element.1277, s32[1]{0:T(128)} %bitcast.405, s32[1]{0:T(128)} %bitcast.406, s32[1]{0:T(128)} %bitcast.407, s32[1]{0:T(128)} %bitcast.408), kind=kLoop, calls=%fused_computation.277.clone.1 | loop fusion | flops 27 | bytes 33 | tf_op jit(solution)/shard_map/vmap(vmap())/scatter
  96.1 2.0 %dynamic-slice_select_fusion.2 = f32[1,2,128,256]{3,2,1,0:T(8,128)S(1)} fusion(f32[2,2,128,256]{3,2,1,0:T(8,128)S(1)} %get-tuple-element.1275, s32[]{:T(128)} %get-tuple-element.1265, f32[2,2,256,256]{3,2,1,0:T(8,128)S(1)} %get-tuple-element.1266, s32[]{:T(128)} %bitcast.403, s32[]{:T(128)} %bitcast.404, pred[]{:T(512)} %and_reduce_fusion.2), kind=kLoop, calls=%fused_computation.276.clone.1 | loop fusion | flops 65536 | bytes 786445 | tf_op jit(solution)/shard_map/vmap(vmap())/scatter
  98.0 2.2 %dynamic-update-slice.3 = f32[2,2,256,256]{3,2,1,0:T(8,128)S(1)} dynamic-update-slice(f32[2,2,256,256]{3,2,1,0:T(8,128)S(1)} %get-tuple-element.1266, f32[1,2,128,256]{3,2,1,0:T(8,128)S(1)} %dynamic-slice_select_fusion.2, s32[]{:T(128)} %bitcast.403, s32[]{:T(128)} %constant.93.clone.1..sunk, s32[]{:T(128)} %bitcast.404, s32[]{:T(128)} %constant.93.clone.1..sunk) | dynamic-update-slice | bytes 524292 | tf_op jit(solution)/shard_map/vmap(vmap())/scatter
  100.6 1.5 %dynamic_update_slice.12 = f32[2,2,128,512]{3,2,1,0:T(8,128)S(1)} dynamic-update-slice(f32[2,2,128,512]{3,2,1,0:T(8,128)S(1)} %broadcast_in_dim.44, f32[2,2,128,128]{3,2,1,0:T(8,128)S(1)} %pad_maximum_fusion.7, s32[]{:T(128)} %constant.93.clone.1, s32[]{:T(128)} %constant.93.clone.1, s32[]{:T(128)} %constant.93.clone.1, s32[]{:T(128)S(6)} %select_n.152) | dynamic-update-slice | bytes 524292 | tf_op jit(solution)/shard_map/dynamic_update_slice | solution.py:108
  102.1 15.0 %collective-permute-done.5 = f32[2,2,128,256]{3,2,0,1:T(8,128)S(1)} collective-permute-done((f32[2,2,128,256]{3,2,0,1:T(8,128)S(1)}, f32[2,2,128,256]{3,2,0,1:T(8,128)S(1)}, u32[]{:S(2)}, u32[]{:S(2)}) %collective-permute-start.5) | collective-permute-done | bytes 524320 | tf_op jit(solution)/shard_map/ppermute | solution.py:11
  117.3 1.5 %dynamic_update_slice.13 = f32[2,2,128,512]{3,2,1,0:T(8,128)S(1)} dynamic-update-slice(f32[2,2,128,512]{3,2,1,0:T(8,128)S(1)} %dynamic_update_slice.12, f32[2,2,128,128]{3,2,1,0:T(8,128)S(1)} %maximum_add_fusion, s32[]{:T(128)} %constant.93.clone.1, s32[]{:T(128)} %constant.93.clone.1, s32[]{:T(128)} %constant.93.clone.1, s32[]{:T(128)S(6)} %select_n.153) | dynamic-update-slice | bytes 524292 | tf_op jit(solution)/shard_map/dynamic_update_slice | solution.py:108
  119.9 1.5 %dynamic_update_slice.15 = f32[2,2,128,512]{3,2,1,0:T(8,128)S(1)} dynamic-update-slice(f32[2,2,128,512]{3,2,1,0:T(8,128)S(1)} %dynamic_update_slice.14, f32[2,2,128,128]{3,2,1,0:T(8,128)S(1)} %maximum_add_fusion.2, s32[]{:T(128)} %constant.93.clone.1, s32[]{:T(128)} %constant.93.clone.1, s32[]{:T(128)} %constant.93.clone.1, s32[]{:T(128)S(6)} %select_n.155) | dynamic-update-slice | bytes 524292 | tf_op jit(solution)/shard_map/dynamic_update_slice | solution.py:108
  121.4 0.9 convert_element_type.118
  (160 shorter events, 26.1 us)
Async XLA Ops:
  0.0 13.5 %copy-start = (f32[2,128,128]{2,1,0:T(8,128)S(1)}, f32[2,128,128]{2,1,0:T(8,128)}, u32[]{:S(2)}) copy-start(f32[2,128,128]{2,1,0:T(8,128)} %param.21) | copy-start | bytes 393220
  0.0 1.4 %copy-start.8 = (s32[16]{0:T(128)S(1)}, s32[16]{0:T(128)}, u32[]{:S(2)}) copy-start(s32[16]{0:T(128)} %param.23) | copy-start | bytes 196
  3.1 12.3 %collective-permute-start.2 = (bf16[2,2,128,256]{2,0,3,1:T(2,128)(2,1)S(1)}, bf16[2,2,128,256]{2,0,3,1:T(2,128)(2,1)S(1)}, u32[]{:S(2)}, u32[]{:S(2)}) collective-permute-start(bf16[2,2,128,256]{2,0,3,1:T(2,128)(2,1)S(1)} %maximum_bitcast_fusion.37), channel_id=1, source_target_pairs={{0,28},{4,0},{8,4},{12,8},{16,12},{20,16},{24,20},{28,24},{1,29},{... | collective-permute-start | bytes 786440 | tf_op jit(solution)/shard_map/ppermute | solution.py:11
  11.3 0.7 copy-start.10
  12.1 0.8 copy-start.5
  13.6 1.4 %copy-start.6 = (f32[128,128]{1,0:T(8,128)S(1)}, f32[128,128]{1,0:T(8,128)}, u32[]{:S(2)}) copy-start(f32[128,128]{1,0:T(8,128)} %param.20) | copy-start | bytes 196612
  13.6 0.7 copy-start.9
  18.6 8.1 %collective-permute-start.3 = (bf16[2,1,128,256]{3,2,0,1:T(8,128)(2,1)S(1)}, bf16[2,1,128,256]{3,2,0,1:T(8,128)(2,1)S(1)}, u32[]{:S(2)}, u32[]{:S(2)}) collective-permute-start(bf16[2,1,128,256]{3,2,0,1:T(8,128)(2,1)S(1)} %bitcast.413), channel_id=1, source_target_pairs={{0,1},{1,0},{2,3},{3,2},{4,5},{5,4},{6,7},{7,6},{8,9},{9,8},{10,11... | collective-permute-start | bytes 393224 | tf_op jit(solution)/shard_map/ppermute | solution.py:21
  27.0 6.8 %collective-permute-start = (f32[1,128,256]{1,2,0:T(8,128)S(1)}, f32[1,128,256]{1,2,0:T(8,128)S(1)}, u32[]{:S(2)}, u32[]{:S(2)}) collective-permute-start(f32[1,128,256]{1,2,0:T(8,128)S(1)} %get-tuple-element.1180), channel_id=1, source_target_pairs={{0,2},{1,3},{4,6},{5,7},{8,10},{9,11},{12,14},{13,15},{16,18},{17,... | collective-permute-start | bytes 393224 | tf_op jit(solution)/shard_map/while/body/eval_jaxpr/ppermute | solution.py:27
  40.9 0.7 copy-start.3
  41.5 0.9 copy-start.4
  42.5 4.1 %collective-permute-start = (f32[1,128,256]{1,2,0:T(8,128)S(1)}, f32[1,128,256]{1,2,0:T(8,128)S(1)}, u32[]{:S(2)}, u32[]{:S(2)}) collective-permute-start(f32[1,128,256]{1,2,0:T(8,128)S(1)} %get-tuple-element.1180), channel_id=1, source_target_pairs={{0,2},{1,3},{4,6},{5,7},{8,10},{9,11},{12,14},{13,15},{16,18},{17,... | collective-permute-start | bytes 393224 | tf_op jit(solution)/shard_map/while/body/eval_jaxpr/ppermute | solution.py:27
  46.9 15.3 %collective-permute-start.1 = (f32[1,128,256]{1,2,0:T(8,128)S(1)}, f32[1,128,256]{1,2,0:T(8,128)S(1)}, u32[]{:S(2)}, u32[]{:S(2)}) collective-permute-start(f32[1,128,256]{1,2,0:T(8,128)S(1)} %get-tuple-element.1228), channel_id=1, source_target_pairs={{2,0},{3,1},{6,4},{7,5},{10,8},{11,9},{14,12},{15,13},{18,16},{19,... | collective-permute-start | bytes 393224 | tf_op jit(solution)/shard_map/while/body/eval_jaxpr/ppermute | solution.py:27
  62.3 12.5 %collective-permute-start.1 = (f32[1,128,256]{1,2,0:T(8,128)S(1)}, f32[1,128,256]{1,2,0:T(8,128)S(1)}, u32[]{:S(2)}, u32[]{:S(2)}) collective-permute-start(f32[1,128,256]{1,2,0:T(8,128)S(1)} %get-tuple-element.1228), channel_id=1, source_target_pairs={{2,0},{3,1},{6,4},{7,5},{10,8},{11,9},{14,12},{15,13},{18,16},{19,... | collective-permute-start | bytes 393224 | tf_op jit(solution)/shard_map/while/body/eval_jaxpr/ppermute | solution.py:27
  80.2 0.7 copy-start.1
  80.9 0.9 copy-start.2
  82.1 1.4 %collective-permute-start.4 = (bf16[2,1,128,256]{3,2,0,1:T(8,128)(2,1)S(1)}, bf16[2,1,128,256]{3,2,0,1:T(8,128)(2,1)S(1)}, u32[]{:S(2)}, u32[]{:S(2)}) collective-permute-start(bf16[2,1,128,256]{3,2,0,1:T(8,128)(2,1)S(1)} %select_convert_fusion), channel_id=1, source_target_pairs={{0,1},{1,0},{2,3},{3,2},{4,5},{5,4},{6,7},{7,6},{8,9},{9,8},{10,11... | collective-permute-start | bytes 393224 | tf_op jit(solution)/shard_map/ppermute | solution.py:21
  83.6 0.7 copy-start.7
  100.3 16.8 %collective-permute-start.5 = (f32[2,2,128,256]{3,2,0,1:T(8,128)S(1)}, f32[2,2,128,256]{3,2,0,1:T(8,128)S(1)}, u32[]{:S(2)}, u32[]{:S(2)}) collective-permute-start(f32[2,2,128,256]{3,2,0,1:T(8,128)S(1)} %slice.693), channel_id=1, source_target_pairs={{0,4},{4,8},{8,12},{12,16},{16,20},{20,24},{24,28},{28,0},{1,5},{5... | collective-permute-start | bytes 1572872 | tf_op jit(solution)/shard_map/ppermute | solution.py:11
where the time goes:
time: 123 us; the launch traced here: 122 us
  waiting for transfers between devices  47.7 us (39%)
  local copies, waits for them, and re-layouts  25 us (20%)
  other arithmetic  15.5 us (13%)
  starting transfers between devices  13.6 us (11%)
  matrix products  11.3 us (9%)
  between operations  8.34 us (7%)
    ppermute x4, waiting for transfers between devices, from_behind_2(): return lax.ppermute(value, axis, pairs)  31.4 us
    ppermute x2, waiting for transfers between devices, from_behind(): lax.ppermute(value, axis, [(i, (i + by) % peers) for i in range(peers)])  15 us
    scatter x4, other arithmetic  10.5 us
    ppermute x4, starting transfers between devices, from_behind_2(): return lax.ppermute(value, axis, pairs)  7.31 us
    ppermute x2, starting transfers between devices, from_behind(): lax.ppermute(value, axis, [(i, (i + by) % peers) for i in range(peers)])  6.12 us
    dot_general x14, matrix products, transform_all(): jnp.einsum('ka,pab->pkb', left_table, first_pass, precision=lax.Precision...  5.79 us
    dot_general x14, matrix products, transform_all(): jnp.dot(flat, right_table, precision=lax.Precision.HIGHEST, preferred_ele...  5.52 us
    scatter x6, local copies, waits for them, and re-layouts  5.5 us
  transfers between devices with their start and end apart: 8, of which 6 were waited for; matrix products, arithmetic and copies ran while one was open for 5% of the time, Pallas kernels for 0%

commit v1 on v0

v1 whole, which is shorter than its diff:
```python
import functools
import math

import jax
import jax.numpy as jnp
import numpy as np
from jax import lax
from jax.experimental import pallas as pl
from jax.experimental.pallas import tpu as pltpu
from jax.sharding import PartitionSpec as P

F32 = jnp.float32
BF16 = jnp.bfloat16


def fourier_parts(window):
    index = np.arange(window)
    angle = (index[:, None] * index[None, :] % window) * (-2.0 * math.pi / window)
    real = np.cos(angle) / math.sqrt(window)
    imag = np.sin(angle) / math.sqrt(window)
    big = np.block([[real, imag], [-imag, real]]).astype(np.float32)
    high = big.astype(BF16)
    low = (big - high.astype(np.float32)).astype(BF16)
    right = np.concatenate([high, high, low], axis=0)
    left = np.concatenate([high.T, high.T, low.T], axis=1)
    return right, left


def split(value):
    high = value.astype(BF16)
    return high, (value - high.astype(F32)).astype(BF16)


def transform(field, right, left, window):
    count = len(field)
    high, low = split(
        jnp.concatenate([jnp.concatenate([re, im], axis=1) for re, im in field], axis=0)
    )
    first = jnp.dot(
        jnp.concatenate([high, low, high], axis=1), right[...], preferred_element_type=F32
    )
    rows = [first[p * window : (p + 1) * window] for p in range(count)]
    high, low = split(
        jnp.concatenate(
            [jnp.concatenate([r[:, :window], r[:, window:]], axis=0) for r in rows], axis=1
        )
    )
    second = jnp.dot(
        left[...], jnp.concatenate([high, low, high], axis=0), preferred_element_type=F32
    )
    out = []
    for p in range(count):
        block = second[:, p * window : (p + 1) * window]
        out.append((block[:window], block[window:]))
    return out


def times(a, b):
    return a[0] * b[0] - a[1] * b[1], a[0] * b[1] + a[1] * b[0]


def conj_times(a, b):
    return a[0] * b[0] + a[1] * b[1], a[0] * b[1] - a[1] * b[0]


def conj(a):
    return a[0], -a[1]


def load(ref, lead, count, window):
    out = []
    for p in range(count):
        block = ref[lead, p].astype(F32)
        out.append((block[:, :window], block[:, window:]))
    return out


def store(ref, lead, field):
    for p, (re, im) in enumerate(field):
        ref[lead, p] = jnp.concatenate([re, im], axis=1).astype(ref.dtype)


def chain(patches, probe, phase, measured, right, left, psi, work, terms, layers):
    slices, count, window = patches.shape[0], patches.shape[1], probe.shape[1]
    first_own = lax.axis_index("slab") * layers
    prop = (jnp.cos(phase[...]), jnp.sin(phase[...]))
    prop_store = work.at[count]
    prop_store[...] = jnp.concatenate(prop, axis=1)

    def propagator():
        value = prop_store[...]
        return value[:, :window], value[:, window:]

    run = functools.partial(transform, right=right, left=left, window=window)
    start = (probe[0].astype(F32), probe[1].astype(F32))
    store(psi, 0, [start] * count)

    def forward(j, carried):
        chi = [
            times(a, b)
            for a, b in zip(load(psi, j, count, window), load(patches, j, count, window))
        ]
        moved = run(chi)
        prop = propagator()
        back = run([conj(times(prop, f)) for f in moved])
        store(psi, j + 1, [conj(f) for f in back])
        return carried

    lax.fori_loop(0, slices - 1, forward, 0)
    last = slices - 1
    chi = [
        times(a, b)
        for a, b in zip(load(psi, last, count, window), load(patches, last, count, window))
    ]
    far = run(chi)
    shaped = []
    for p, (re, im) in enumerate(far):
        misfit = re * re + im * im - measured[p]
        shaped.append((misfit * re, -(misfit * im)))
    grad = [conj(f) for f in run(shaped)]
    for p in range(count):
        work[p] = jnp.concatenate(grad[p], axis=1)

    def own_term(j):
        @pl.when((j >= first_own) & (j < first_own + layers))
        def _():
            for p in range(count):
                block = work[p]
                wave = psi[j, p]
                term = conj_times(
                    (wave[:, :window], wave[:, window:]), (block[:, :window], block[:, window:])
                )
                terms[j - first_own, p] = jnp.concatenate(term, axis=1)

    def backward(i, carried):
        j = last - i
        own_term(j)
        grads = []
        for p in range(count):
            block = work[p]
            grads.append((block[:, :window], block[:, window:]))
        inner = [conj_times(a, b) for a, b in zip(load(patches, j, count, window), grads)]
        moved = run(inner)
        prop = propagator()
        back = run([conj(conj_times(prop, f)) for f in moved])
        for p in range(count):
            work[p] = jnp.concatenate(conj(back[p]), axis=1)
        return carried

    lax.fori_loop(0, last, backward, 0)
    own_term(0)


def chain_kernel(patches, probe, phase, measured, right, left, terms, psi, work):
    chain(patches, probe, phase, measured, right, left, psi, work, terms, terms.shape[0])


def body(object_field, probe_wave, prop_phase, intensity, patch_rows, patch_cols):
    window = probe_wave.shape[1]
    layers = object_field.shape[1]
    columns = object_field.shape[3]
    count = intensity.shape[0]
    tiles = lax.axis_size("tile")
    sections = lax.axis_size("slab")
    slices = sections * layers
    here = lax.axis_index("tile")
    before = (here + tiles - 1) % tiles
    own_rows = lax.dynamic_slice_in_dim(patch_rows, here * count, count)
    own_cols = lax.dynamic_slice_in_dim(patch_cols, here * count, count)
    prior_cols = lax.dynamic_slice_in_dim(patch_cols, before * count, count)
    right, left = fourier_parts(window)

    def column_pick(cols):
        at = cols[:, None] + jnp.arange(window, dtype=jnp.int32)[None, :]
        return jnp.arange(columns, dtype=jnp.int32)[:, None, None] == at[None]

    def cut(cols):
        return jnp.einsum(
            "zlrc,cpk->lprzk", object_field, column_pick(cols).astype(BF16)
        ).reshape(layers, count, window, 2 * window)

    def shift(value, by):
        peers = lax.axis_size("tile")
        return lax.ppermute(value, "tile", [(i, (i + by) % peers) for i in range(peers)])

    arrived = shift(cut(prior_cols), -1)
    stacked = jnp.concatenate([cut(own_cols), arrived], axis=2)
    row_at = own_rows[:, None] + jnp.arange(window, dtype=jnp.int32)[None, :]
    row_pick = jnp.arange(2 * window, dtype=jnp.int32)[None, None, :] == row_at[:, :, None]
    mine = jnp.einsum("pir,lprk->lpik", row_pick.astype(BF16), stacked)
    patches = lax.all_gather(mine, "slab", axis=0, tiled=True)
    terms = pl.pallas_call(
        chain_kernel,
        out_shape=jax.ShapeDtypeStruct((layers, count, window, 2 * window), F32),
        in_specs=[pl.BlockSpec(memory_space=pltpu.VMEM)] * 6,
        out_specs=pl.BlockSpec(memory_space=pltpu.VMEM),
        scratch_shapes=[
            pltpu.VMEM((slices, count, window, 2 * window), F32),
            pltpu.VMEM((count + 1, window, 2 * window), F32),
        ],
        compiler_params=pltpu.CompilerParams(vmem_limit_bytes=60 * 1024 * 1024),
    )(patches, probe_wave, prop_phase, intensity, jnp.asarray(right), jnp.asarray(left))
    placed = jnp.einsum(
        "pir,lpik->lprk", row_pick.astype(F32), terms, precision=lax.Precision.HIGH
    )
    received = shift(placed[:, :, window:].astype(BF16), 1)
    pieces = jnp.concatenate([placed[:, :, :window], received.astype(F32)], axis=1)
    picks = jnp.concatenate([column_pick(own_cols), column_pick(prior_cols)], axis=1)
    gradient = jnp.einsum(
        "lprzk,cpk->zlrc",
        pieces.reshape(layers, 2 * count, window, 2, window),
        picks.astype(F32),
        precision=lax.Precision.HIGH,
    )
    return gradient.astype(BF16)


def solution(mesh):
    return jax.shard_map(
        body,
        mesh=mesh,
        in_specs=(P(None, "slab", "tile", None), P(), P(), P("tile", None, None), P(), P()),
        out_specs=P(None, "slab", "tile", None),
        check_vma=False,
    )
```

time: 123 us -> 84.8 us (0.69)
  Pallas kernels: 0 us -> 22.4 us
  local copies, waits for them, and re-layouts: 25 us -> 4.62 us
  other arithmetic: 15.5 us -> 0.41 us
  waiting for transfers between devices: 47.7 us -> 32.7 us
  matrix products: 11.3 us -> 3.38 us
  starting transfers between devices: 13.6 us -> 7.58 us
  between operations: 8.34 us -> 13.5 us
    ppermute x8 -> x2, waiting for transfers between devices: 47.7 us -> 13.9 us  [shift(): lax.ppermute(value, 'tile', [(i, (i + by) % peers) for i in range(peers)])]
    pallas_call x0 -> x1, Pallas kernels: none -> 22.4 us  [body(): pl.pallas_call(chain_kernel, out_shape=jax.ShapeDtypeStruct((layers, coun...]
    all_gather x0 -> x1, waiting for transfers between devices: none -> 18.8 us  [body(): patches = lax.all_gather(mine, 'slab', axis=0, tiled=True)]
    scatter x5 -> x0, other arithmetic: 10.5 us -> none
    dot_general x28 -> x3, matrix products: 11.3 us -> 2.69 us  [the longest x1 1.57 us: body(): jnp.einsum('pir,lpik->lprk', row_pick.astype(F32), terms, precision=lax.P...]
    ppermute x8 -> x2, starting transfers between devices: 13.6 us -> 7.57 us  [shift(): lax.ppermute(value, 'tile', [(i, (i + by) % peers) for i in range(peers)])]
    scatter x6 -> x0, local copies, waits for them, and re-layouts: 5.5 us -> none
    dynamic_update_slice x4 -> x0, local copies, waits for them, and re-layouts: 5.21 us -> none  [add_block(): return lax.dynamic_update_slice(gradient, current + paired, where_at)]
  transfers between devices with their start and end apart: 8 -> 3, of which waited for: 6 -> 3; matrix products, arithmetic and copies ran while one was open for 5% -> 1% of each run, Pallas kernels for 0% -> 0%
where the time goes in v1:
time: 84.8 us; the launch traced here: 84.5 us
  waiting for transfers between devices  32.7 us (39%)
  Pallas kernels  22.4 us (26%)
  between operations  13.5 us (16%)
  starting transfers between devices  7.58 us (9%)
  local copies, waits for them, and re-layouts  4.62 us (5%)
  matrix products  3.38 us (4%)
    pallas_call x1, Pallas kernels, body(): pl.pallas_call(chain_kernel, out_shape=jax.ShapeDtypeStruct((layers, coun...  22.4 us
    all_gather x1, waiting for transfers between devices, body(): patches = lax.all_gather(mine, 'slab', axis=0, tiled=True)  18.8 us
    ppermute x2, waiting for transfers between devices, shift(): lax.ppermute(value, 'tile', [(i, (i + by) % peers) for i in range(peers)])  13.9 us
    ppermute x2, starting transfers between devices, shift(): lax.ppermute(value, 'tile', [(i, (i + by) % peers) for i in range(peers)])  7.57 us
  transfers between devices with their start and end apart: 3, of which 3 were waited for; matrix products, arithmetic and copies ran while one was open for 1% of the time, Pallas kernels for 0%

profile of v1, /device:TPU:0, one launch (start us, length us, event | category | flops | bytes accessed | tf_op | source)
XLA Modules:
  0.0 84.5 jit_solution(16258320308589782573)
XLA Ops:
  6.5 0.0 copy-start
  6.5 0.0 all-gather.2.cloned.1.call-start
  6.5 0.0 copy-start.2
  6.5 0.7 copy-done.2
  7.3 0.1 fusion.22
  7.3 0.1 iota_add_fusion.1
  7.4 0.2 copy-done
  7.6 0.3 fusion.3
  8.0 6.1 %collective-permute-start = (bf16[2,2,128,256]{2,3,1,0:T(8,128)(2,1)S(1)}, bf16[2,2,128,256]{2,3,1,0:T(8,128)(2,1)S(1)}, u32[]{:S(2)}, u32[]{:S(2)}) collective-permute-start(bf16[2,2,128,256]{2,3,1,0:T(8,128)(2,1)S(1)} %bitcast.53), channel_id=1, source_target_pairs={{0,28},{4,0},{8,4},{12,8},{16,12},{20,16},{24,20},{28,24},{1,29},{... | collective-permute-start | bytes 786440 | tf_op jit(solution)/shard_map/ppermute | solution.py:184
  14.0 0.3 fusion.2
  14.4 0.0 copy-start.3
  14.4 0.6 copy-done.3
  15.0 0.1 dynamic_slice.11
  15.1 0.1 iota_add_fusion
  15.2 4.4 %collective-permute-done = bf16[2,2,128,256]{2,3,1,0:T(8,128)(2,1)S(1)} collective-permute-done((bf16[2,2,128,256]{2,3,1,0:T(8,128)(2,1)S(1)}, bf16[2,2,128,256]{2,3,1,0:T(8,128)(2,1)S(1)}, u32[]{:S(2)}, u32[]{:S(2)}) %collective-permute-start) | collective-permute-done | bytes 262176 | tf_op jit(solution)/shard_map/ppermute | solution.py:184
  19.6 0.4 convolution_bitcast_fusion.2
  20.0 0.9 %copy.25 = bf16[2,2,128,256]{3,2,1,0:T(8,128)(2,1)} copy(bf16[2,2,128,256]{2,3,1,0:T(8,128)(2,1)S(1)} %convolution_bitcast_fusion.2) | data formatting | bytes 524288 | tf_op jit(solution)/shard_map/pir,lprk->lpik/transpose | solution.py:190
  20.8 0.0 all-gather.2.cloned.1.call-update
  20.9 18.8 %all-gather.2.cloned.1.call-done.patches = bf16[8,2,128,256]{3,2,1,0:T(8,128)(2,1)} async-done(((bf16[2,2,128,256]{3,2,1,0:T(8,128)(2,1)}), bf16[8,2,128,256]{3,2,1,0:T(8,128)(2,1)}) %all-gather.2.cloned.1.call-update) | async-done | bytes 1048592 | tf_op jit(solution)/shard_map/all_gather | solution.py:191
  39.6 22.4 %shard_map.82 = f32[2,2,128,256]{3,2,1,0:T(8,128)} custom-call(bf16[8,2,128,256]{3,2,1,0:T(8,128)(2,1)} %all-gather.2.cloned.1.call-done.patches, bf16[2,128,128]{2,1,0:T(8,128)(2,1)} %probe.1, f32[128,128]{1,0:T(8,128)} %phase.1, f32[2,128,128]{2,1,0:T(8,128)} %measured.1, bf16[768,256]{1,0:T(8,128)(2,1)} %constant.31.clone.right, ...), custom_call_target="tpu_custom_call" | custom-call | tf_op jit(solution)/shard_map/pallas_call | solution.py:192
  62.0 1.6 %convolution_bitcast_fusion = f32[2,2,256,256]{2,3,0,1:T(8,128)S(1)} fusion(f32[2,2,128,256]{3,2,1,0:T(8,128)} %shard_map.82, s32[2,128]{1,0:T(2,128)S(1)} %iota_add_fusion), kind=kOutput, calls=%fused_computation | convolution fusion | flops 201392128 | bytes 1573888 | tf_op jit(solution)/shard_map/pir,lpik->lprk/dot_general | solution.py:203
  63.6 0.0 copy-start.1
  63.6 1.5 %collective-permute-start.1 = (bf16[2,2,128,256]{2,3,0,1:T(8,128)(2,1)S(1)}, bf16[2,2,128,256]{2,3,0,1:T(8,128)(2,1)S(1)}, u32[]{:S(2)}, u32[]{:S(2)}) collective-permute-start(bf16[2,2,128,256]{2,3,0,1:T(8,128)(2,1)S(1)} %slice.12), channel_id=1, source_target_pairs={{0,4},{4,8},{8,12},{12,16},{16,20},{20,24},{24,28},{28,0},{1,5},{5... | collective-permute-start | bytes 786440 | tf_op jit(solution)/shard_map/ppermute | solution.py:184
  65.1 0.1 iota_compare_fusion
  65.2 0.1 iota_compare_fusion.1
  65.3 0.0 copy-done.1
  65.3 9.5 %collective-permute-done.1 = bf16[2,2,128,256]{2,3,0,1:T(8,128)(2,1)S(1)} collective-permute-done((bf16[2,2,128,256]{2,3,0,1:T(8,128)(2,1)S(1)}, bf16[2,2,128,256]{2,3,0,1:T(8,128)(2,1)S(1)}, u32[]{:S(2)}, u32[]{:S(2)}) %collective-permute-start.1) | collective-permute-done | bytes 262176 | tf_op jit(solution)/shard_map/ppermute | solution.py:184
  74.8 0.0 slice-start
  74.9 1.0 %slice-done = f32[2,2,128,256]{2,3,0,1:T(8,128)S(1)} async-done(((f32[2,2,256,256]{2,3,0,1:T(8,128)}), f32[2,2,128,256]{2,3,0,1:T(8,128)S(1)}, s32[]{:S(2)}) %slice-start) | async-done | bytes 524312 | tf_op jit(solution)/shard_map/slice | solution.py:207
  75.9 0.1 pad_maximum_fusion
  75.9 0.7 fusion.1
  76.7 1.0 %copy.28 = bf16[2,2,128,512]{3,2,1,0:T(8,128)(2,1)} copy(bf16[2,2,128,512]{2,3,0,1:T(8,128)(2,1)S(1)} %fusion.1) | data formatting | bytes 1048576 | tf_op jit(solution)/shard_map/convert_element_type | solution.py:215
  (4 shorter events, 0.1 us)
Async XLA Ops:
  6.5 1.1 %copy-start = (bf16[2,2,128,512]{3,2,1,0:T(8,128)(2,1)S(1)}, bf16[2,2,128,512]{3,2,1,0:T(8,128)(2,1)}, u32[]{:S(2)}) copy-start(bf16[2,2,128,512]{3,2,1,0:T(8,128)(2,1)} %param.8) | copy-start | bytes 1572868
  6.5 33.1 %all-gather.2.cloned.1.call-start = ((), (), s32[]{:S(2)}) async-start(), calls=%async_computation | async-start | bytes 1310720 | tf_op jit(solution)/shard_map/all_gather | solution.py:191
  6.5 0.7 copy-start.2
  8.0 11.6 %collective-permute-start = (bf16[2,2,128,256]{2,3,1,0:T(8,128)(2,1)S(1)}, bf16[2,2,128,256]{2,3,1,0:T(8,128)(2,1)S(1)}, u32[]{:S(2)}, u32[]{:S(2)}) collective-permute-start(bf16[2,2,128,256]{2,3,1,0:T(8,128)(2,1)S(1)} %bitcast.53), channel_id=1, source_target_pairs={{0,28},{4,0},{8,4},{12,8},{16,12},{20,16},{24,20},{28,24},{1,29},{... | collective-permute-start | bytes 786440 | tf_op jit(solution)/shard_map/ppermute | solution.py:184
  14.4 0.7 copy-start.3
  63.6 1.7 %copy-start.1 = (f32[2,2,256,256]{2,3,0,1:T(8,128)}, f32[2,2,256,256]{2,3,0,1:T(8,128)S(1)}, u32[]{:S(2)}) copy-start(f32[2,2,256,256]{2,3,0,1:T(8,128)S(1)} %convolution_bitcast_fusion) | copy-start | bytes 3145732
  63.6 11.2 %collective-permute-start.1 = (bf16[2,2,128,256]{2,3,0,1:T(8,128)(2,1)S(1)}, bf16[2,2,128,256]{2,3,0,1:T(8,128)(2,1)S(1)}, u32[]{:S(2)}, u32[]{:S(2)}) collective-permute-start(bf16[2,2,128,256]{2,3,0,1:T(8,128)(2,1)S(1)} %slice.12), channel_id=1, source_target_pairs={{0,4},{4,8},{8,12},{12,16},{16,20},{20,24},{24,28},{28,0},{1,5},{5... | collective-permute-start | bytes 786440 | tf_op jit(solution)/shard_map/ppermute | solution.py:184
  74.8 1.0 %slice-start = ((f32[2,2,256,256]{2,3,0,1:T(8,128)}), f32[2,2,128,256]{2,3,0,1:T(8,128)S(1)}, s32[]{:S(2)}) async-start(f32[2,2,256,256]{2,3,0,1:T(8,128)} %copy-done.1), calls=%async_computation.1 | async-start | bytes 1048576 | tf_op jit(solution)/shard_map/slice | solution.py:207
Sparse Core Ops, SparseCore 0:
  21.0 18.5 all-gather.1

commit v2 on v1

v2 whole, which is shorter than its diff:
```python
import functools
import math

import jax
import jax.numpy as jnp
import numpy as np
from jax import lax
from jax.experimental import pallas as pl
from jax.experimental.pallas import tpu as pltpu
from jax.sharding import PartitionSpec as P

F32 = jnp.float32
BF16 = jnp.bfloat16


def fourier_parts(window):
    index = np.arange(window)
    angle = (index[:, None] * index[None, :] % window) * (-2.0 * math.pi / window)
    real = np.cos(angle) / math.sqrt(window)
    imag = np.sin(angle) / math.sqrt(window)
    big = np.block([[real, imag], [-imag, real]]).astype(np.float32)
    high = big.astype(BF16)
    low = (big - high.astype(np.float32)).astype(BF16)
    right = np.concatenate([high, high, low], axis=0)
    left = np.concatenate([high.T, high.T, low.T], axis=1)
    return right, left


def split(value):
    high = value.astype(BF16)
    return high, (value - high.astype(F32)).astype(BF16)


def transform(field, right, left, window):
    count = len(field)
    high, low = split(
        jnp.concatenate([jnp.concatenate([re, im], axis=1) for re, im in field], axis=0)
    )
    first = jnp.dot(
        jnp.concatenate([high, low, high], axis=1), right[...], preferred_element_type=F32
    )
    rows = [first[p * window : (p + 1) * window] for p in range(count)]
    high, low = split(
        jnp.concatenate(
            [jnp.concatenate([r[:, :window], r[:, window:]], axis=0) for r in rows], axis=1
        )
    )
    second = jnp.dot(
        left[...], jnp.concatenate([high, low, high], axis=0), preferred_element_type=F32
    )
    out = []
    for p in range(count):
        block = second[:, p * window : (p + 1) * window]
        out.append((block[:window], block[window:]))
    return out


def times(a, b):
    return a[0] * b[0] - a[1] * b[1], a[0] * b[1] + a[1] * b[0]


def conj_times(a, b):
    return a[0] * b[0] + a[1] * b[1], a[0] * b[1] - a[1] * b[0]


def conj(a):
    return a[0], -a[1]


def load(ref, lead, count, window):
    out = []
    for p in range(count):
        block = ref[lead, p].astype(F32)
        out.append((block[:, :window], block[:, window:]))
    return out


def store(ref, lead, field):
    for p, (re, im) in enumerate(field):
        ref[lead, p] = jnp.concatenate([re, im], axis=1).astype(ref.dtype)


MESH = pl.DeviceIdType.MESH


def one_hot(shape, along, offset):
    here = lax.broadcasted_iota(jnp.int32, shape, along)
    there = lax.broadcasted_iota(jnp.int32, shape, 1 - along)
    return jnp.where(here == there + offset, 1.0, 0.0).astype(BF16)


def halves(block, window):
    return block[:, :window], block[:, window:]


def kernel(
    tiles, sections, row_ref, col_ref, obj, probe, phase, measured, right, left, out,
    cut_prior, cut_own, low, patches, psi, work, terms, spill, spilled,
    tile_send, tile_recv, cross_send, cross_recv, pair_send, pair_recv, back_send, back_recv,
):
    layers, window, columns = obj.shape[1], obj.shape[2], obj.shape[3]
    count, slices = measured.shape[0], patches.shape[0]
    groups = sections // 2
    last = slices - 1
    tile = lax.axis_index("tile")
    slab = lax.axis_index("slab")
    after, prior = lax.rem(tile + 1, tiles), lax.rem(tile + tiles - 1, tiles)
    group, side = slab // 2, lax.rem(slab, 2)
    partner = slab + 1 - 2 * side
    first_own = slab * layers

    def remote(src, dst, send, recv, **device):
        return pltpu.make_async_remote_copy(
            src_ref=src, dst_ref=dst, send_sem=send, recv_sem=recv,
            device_id=device, device_id_type=MESH,
        )

    barrier = pltpu.get_barrier_semaphore()
    greeted = [{"tile": after}, {"tile": prior}, {"slab": partner}]
    for step in range(1, groups):
        greeted.append({"slab": lax.rem(group + step, groups) * 2 + side})
    for device in greeted:
        pl.semaphore_signal(barrier, inc=1, device_id=device, device_id_type=MESH)

    def columns_of(base):
        return [col_ref[base * count + p] for p in range(count)]

    prior_cols, own_cols = columns_of(prior), columns_of(tile)
    own_rows = [row_ref[tile * count + p] for p in range(count)]

    def cut(cols, layer, target):
        pick = jnp.concatenate([one_hot((columns, window), 0, c) for c in cols], axis=1)
        both = jnp.concatenate([obj[0, layer], obj[1, layer]], axis=0)
        got = jnp.dot(both, pick, preferred_element_type=F32).astype(BF16)
        for p in range(count):
            part = got[:, p * window : (p + 1) * window]
            target[layer, p] = jnp.concatenate([part[:window], part[window:]], axis=1)

    def tile_copy(layer):
        return remote(
            cut_prior.at[layer], low.at[layer], tile_send.at[layer], tile_recv.at[layer], tile=prior
        )

    for layer in range(layers):
        cut(prior_cols, layer, cut_prior)
    pl.semaphore_wait(barrier, len(greeted))
    for layer in range(layers):
        tile_copy(layer).start()
    for layer in range(layers):
        cut(own_cols, layer, cut_own)
    work[count] = jnp.concatenate([jnp.cos(phase[...]), jnp.sin(phase[...])], axis=1)

    def cross_copy(step, layer):
        block = patches.at[first_own + layer]
        return remote(
            block, block, cross_send.at[step - 1, layer], cross_recv.at[step - 1, layer],
            slab=lax.rem(group + step, groups) * 2 + side,
        )

    def origin(step, of_side):
        return (lax.rem(group + groups - step, groups) * 2 + of_side) * layers

    def cross_arrival(step, layer):
        block = patches.at[origin(step, side) + layer]
        return remote(
            block, block, cross_send.at[step - 1, layer], cross_recv.at[step - 1, layer],
            slab=lax.rem(group + step, groups) * 2 + side,
        )

    def pair_copy(step, layer):
        block = patches.at[origin(step, side) + layer]
        return remote(
            block, block, pair_send.at[step, layer], pair_recv.at[step, layer], slab=partner
        )

    def pair_arrival(step, layer):
        block = patches.at[origin(step, 1 - side) + layer]
        return remote(
            block, block, pair_send.at[step, layer], pair_recv.at[step, layer], slab=partner
        )

    for layer in range(layers):
        tile_copy(layer).wait_recv()
        for p in range(count):
            both = jnp.concatenate([cut_own[layer, p], low[layer, p]], axis=0)
            pick = one_hot((window, 2 * window), 1, own_rows[p])
            patches[first_own + layer, p] = jnp.dot(
                pick, both, preferred_element_type=F32
            ).astype(BF16)
        for step in range(1, groups):
            cross_copy(step, layer).start()
        pair_copy(0, layer).start()
    for layer in range(layers):
        for step in range(1, groups):
            cross_arrival(step, layer).wait_recv()
            pair_copy(step, layer).start()
    for layer in range(layers):
        for step in range(groups):
            pair_arrival(step, layer).wait_recv()

    run = functools.partial(transform, right=right, left=left, window=window)
    start = (probe[0].astype(F32), probe[1].astype(F32))
    store(psi, 0, [start] * count)

    def propagator():
        return halves(work[count], window)

    def forward(j, carried):
        chi = [
            times(a, b)
            for a, b in zip(load(psi, j, count, window), load(patches, j, count, window))
        ]
        moved = run(chi)
        prop = propagator()
        back = run([conj(times(prop, f)) for f in moved])
        store(psi, j + 1, [conj(f) for f in back])
        return carried

    lax.fori_loop(0, last, forward, 0)
    chi = [
        times(a, b)
        for a, b in zip(load(psi, last, count, window), load(patches, last, count, window))
    ]
    far = run(chi)
    shaped = []
    for p, (re, im) in enumerate(far):
        misfit = re * re + im * im - measured[p]
        shaped.append((misfit * re, -(misfit * im)))
    grad = [conj(f) for f in run(shaped)]
    for p in range(count):
        work[p] = jnp.concatenate(grad[p], axis=1)

    def spill_copy(layer):
        return remote(
            spill.at[layer], spilled.at[layer], back_send.at[layer], back_recv.at[layer], tile=after
        )

    def own_term(j):
        @pl.when((j >= first_own) & (j < first_own + layers))
        def _():
            layer = j - first_own
            for p in range(count):
                term = jnp.concatenate(
                    conj_times(halves(psi[j, p], window), halves(work[p], window)), axis=1
                )
                pick = one_hot((2 * window, window), 0, own_rows[p])
                placed = jnp.dot(
                    jnp.concatenate([pick, pick], axis=1),
                    jnp.concatenate(split(term), axis=0),
                    preferred_element_type=F32,
                )
                terms[layer, p] = placed[:window]
                spill[layer, p] = placed[window:].astype(BF16)
            spill_copy(layer).start()

    def backward(i, carried):
        j = last - i
        own_term(j)
        grads = [halves(work[p], window) for p in range(count)]
        inner = [conj_times(a, b) for a, b in zip(load(patches, j, count, window), grads)]
        moved = run(inner)
        prop = propagator()
        back = run([conj(conj_times(prop, f)) for f in moved])
        for p in range(count):
            work[p] = jnp.concatenate(conj(back[p]), axis=1)
        return carried

    lax.fori_loop(0, last, backward, 0)
    own_term(0)

    own_place = jnp.concatenate([one_hot((window, columns), 1, c) for c in own_cols], axis=0)
    prior_place = jnp.concatenate([one_hot((window, columns), 1, c) for c in prior_cols], axis=0)

    def by_part(ref, layer):
        wide = [halves(ref[layer, p], window) for p in range(count)]
        return jnp.concatenate(
            [jnp.concatenate([w[part] for w in wide], axis=1) for part in range(2)], axis=0
        )

    for layer in reversed(range(layers)):
        high, low_part = split(by_part(terms, layer))
        total = jnp.dot(high, own_place, preferred_element_type=F32)
        total += jnp.dot(low_part, own_place, preferred_element_type=F32)
        spill_copy(layer).wait_recv()
        total += jnp.dot(by_part(spilled, layer), prior_place, preferred_element_type=F32)
        out[0, layer] = total[:window].astype(out.dtype)
        out[1, layer] = total[window:].astype(out.dtype)
    for layer in range(layers):
        tile_copy(layer).wait_send()
        spill_copy(layer).wait_send()
        for step in range(1, groups):
            cross_copy(step, layer).wait_send()
        for step in range(groups):
            pair_copy(step, layer).wait_send()


def body(object_field, probe_wave, prop_phase, intensity, patch_rows, patch_cols):
    window = probe_wave.shape[1]
    layers = object_field.shape[1]
    count = intensity.shape[0]
    tiles, sections = lax.axis_size("tile"), lax.axis_size("slab")
    slices = sections * layers
    groups = sections // 2
    right, left = fourier_parts(window)
    wide = (layers, count, window, 2 * window)
    dma = pltpu.SemaphoreType.DMA
    return pl.pallas_call(
        functools.partial(kernel, tiles, sections),
        out_shape=jax.ShapeDtypeStruct(object_field.shape, BF16),
        in_specs=[pl.BlockSpec(memory_space=pltpu.SMEM)] * 2
        + [pl.BlockSpec(memory_space=pltpu.VMEM)] * 6,
        out_specs=pl.BlockSpec(memory_space=pltpu.VMEM),
        scratch_shapes=[
            pltpu.VMEM(wide, BF16),
            pltpu.VMEM(wide, BF16),
            pltpu.VMEM(wide, BF16),
            pltpu.VMEM((slices,) + wide[1:], BF16),
            pltpu.VMEM((slices,) + wide[1:], F32),
            pltpu.VMEM((count + 1, window, 2 * window), F32),
            pltpu.VMEM(wide, F32),
            pltpu.VMEM(wide, BF16),
            pltpu.VMEM(wide, BF16),
            dma((layers,)),
            dma((layers,)),
            dma((groups - 1, layers)),
            dma((groups - 1, layers)),
            dma((groups, layers)),
            dma((groups, layers)),
            dma((layers,)),
            dma((layers,)),
        ],
        compiler_params=pltpu.CompilerParams(
            collective_id=0, has_side_effects=True, vmem_limit_bytes=60 * 1024 * 1024
        ),
    )(
        patch_rows, patch_cols, object_field, probe_wave, prop_phase, intensity,
        jnp.asarray(right), jnp.asarray(left),
    )


def solution(mesh):
    return jax.shard_map(
        body,
        mesh=mesh,
        in_specs=(P(None, "slab", "tile", None), P(), P(), P("tile", None, None), P(), P()),
        out_specs=P(None, "slab", "tile", None),
        check_vma=False,
    )
```

time: 84.8 us -> 51.2 us (0.60)
  waiting for transfers between devices: 32.7 us -> 0 us
  Pallas kernels: 22.4 us -> 49.2 us
  between operations: 13.5 us -> 0.01 us
  starting transfers between devices: 7.58 us -> 0 us
  matrix products: 3.38 us -> 0 us
  local copies, waits for them, and re-layouts: 4.62 us -> 1.87 us
    pallas_call x1, Pallas kernels: 22.4 us -> 49.2 us  [body(): pl.pallas_call(functools.partial(kernel, tiles, sections), out_shape=jax....]
    all_gather x1 -> x0, waiting for transfers between devices: 18.8 us -> none  [body(): patches = lax.all_gather(mine, 'slab', axis=0, tiled=True)]
    ppermute x2 -> x0, waiting for transfers between devices: 13.9 us -> none  [shift(): lax.ppermute(value, 'tile', [(i, (i + by) % peers) for i in range(peers)])]
    ppermute x2 -> x0, starting transfers between devices: 7.57 us -> none  [shift(): lax.ppermute(value, 'tile', [(i, (i + by) % peers) for i in range(peers)])]
    dot_general x3 -> x0, matrix products: 2.69 us -> none  [the longest x1 1.57 us: body(): jnp.einsum('pir,lpik->lprk', row_pick.astype(F32), terms, precision=lax.P...]
    slice x3 -> x0, local copies, waits for them, and re-layouts: 1.04 us -> none  [the longest x2 1 us: body(): placed[:, :, :window]]
    convert_element_type x1 -> x0, local copies, waits for them, and re-layouts: 1.01 us -> none  [body(): return gradient.astype(BF16)]
    transpose x3 -> x0, local copies, waits for them, and re-layouts: 0.89 us -> none  [the longest x1 0.85 us: body(): mine = jnp.einsum('pir,lprk->lpik', row_pick.astype(BF16), stacked)]
  transfers between devices with their start and end apart: 3 -> 0, of which waited for: 3 -> 0; matrix products, arithmetic and copies ran while one was open for 1% -> 0% of each run, Pallas kernels for 0% -> 0%
where the time goes in v2:
time: 51.2 us; the launch traced here: 51.1 us
  Pallas kernels  49.2 us (96%)
  local copies, waits for them, and re-layouts  1.87 us (4%)
    pallas_call x1, Pallas kernels, body(): pl.pallas_call(functools.partial(kernel, tiles, sections), out_shape=jax....  49.2 us
    unnamed x1, local copies, waits for them, and re-layouts  1.87 us

profile of v2, /device:TPU:0, one launch (start us, length us, event | category | flops | bytes accessed | tf_op | source)
XLA Modules:
  0.0 51.1 jit_solution(3815233666503555309)
XLA Ops:
  0.0 49.2 %shard_map.82 = bf16[2,2,128,512]{3,2,1,0:T(8,128)(2,1)} custom-call(s32[16]{0:T(128)} %row_ref.1, s32[16]{0:T(128)} %col_ref.1, bf16[2,2,128,512]{3,2,1,0:T(8,128)(2,1)} %obj.1, bf16[2,128,128]{2,1,0:T(8,128)(2,1)} %probe.1, f32[128,128]{1,0:T(8,128)} %phase.1, f32[2,128,128]{2,1,0:T(8,128)} %measured.1, bf16[768,256]{1,0:T(8,128)(2,1)} %constant.4.clone.right, ...), custom_call_target="tpu_custom_call" | custom-call | tf_op jit(solution)/shard_map/pallas_call | solution.py:307
  49.2 1.9 %copy.10 = bf16[2,2,128,512]{3,2,1,0:T(8,128)(2,1)} copy(bf16[2,2,128,512]{3,2,1,0:T(8,128)(2,1)} %shard_map.82) | data formatting | bytes 1048576

commit v3 on v2

--- a/solution.py
+++ b/solution.py
@@ -179,7 +179,7 @@
             block, block, pair_send.at[step, layer], pair_recv.at[step, layer], slab=partner
         )
 
-    for layer in range(layers):
+    def take_rows(layer):
         tile_copy(layer).wait_recv()
         for p in range(count):
             both = jnp.concatenate([cut_own[layer, p], low[layer, p]], axis=0)
@@ -187,15 +187,29 @@
             patches[first_own + layer, p] = jnp.dot(
                 pick, both, preferred_element_type=F32
             ).astype(BF16)
+        pair_copy(0, layer).start()
         for step in range(1, groups):
             cross_copy(step, layer).start()
-        pair_copy(0, layer).start()
-    for layer in range(layers):
-        for step in range(1, groups):
+
+    take_rows(0)
+
+    @pl.when(group > 0)
+    def _():
+        for layer in range(1, layers):
+            take_rows(layer)
+
+    def arrive(j):
+        owner, layer = j // layers, lax.rem(j, layers)
+        of_group, of_side = owner // 2, lax.rem(owner, 2)
+        step = lax.rem(group - of_group + groups, groups)
+
+        @pl.when((of_side == side) & (of_group != group))
+        def _():
             cross_arrival(step, layer).wait_recv()
             pair_copy(step, layer).start()
-    for layer in range(layers):
-        for step in range(groups):
+
+        @pl.when(of_side != side)
+        def _():
             pair_arrival(step, layer).wait_recv()
 
     run = functools.partial(transform, right=right, left=left, window=window)
@@ -206,6 +220,11 @@
         return halves(work[count], window)
 
     def forward(j, carried):
+        @pl.when((group == 0) & (j >= 1) & (j < layers))
+        def _():
+            take_rows(j)
+
+        arrive(j)
         chi = [
             times(a, b)
             for a, b in zip(load(psi, j, count, window), load(patches, j, count, window))
@@ -217,6 +236,7 @@
         return carried
 
     lax.fori_loop(0, last, forward, 0)
+    arrive(last)
     chi = [
         times(a, b)
         for a, b in zip(load(psi, last, count, window), load(patches, last, count, window))
@@ -265,8 +285,8 @@
             work[p] = jnp.concatenate(conj(back[p]), axis=1)
         return carried
 
-    lax.fori_loop(0, last, backward, 0)
-    own_term(0)
+    lax.fori_loop(0, last - first_own, backward, 0)
+    own_term(first_own)
 
     own_place = jnp.concatenate([one_hot((window, columns), 1, c) for c in own_cols], axis=0)
     prior_place = jnp.concatenate([one_hot((window, columns), 1, c) for c in prior_cols], axis=0)

time: 51.2 us -> 46.1 us (0.900)
  Pallas kernels: 49.2 us -> 44 us
    pallas_call x1, Pallas kernels: 49.2 us -> 44 us  [body(): pl.pallas_call(functools.partial(kernel, tiles, sections), out_shape=jax....]
where the time goes in v3:
time: 46.1 us; the launch traced here: 45.9 us
  Pallas kernels  44 us (95%)
  local copies, waits for them, and re-layouts  1.87 us (4%)
    pallas_call x1, Pallas kernels, body(): pl.pallas_call(functools.partial(kernel, tiles, sections), out_shape=jax....  44 us
    unnamed x1, local copies, waits for them, and re-layouts  1.87 us

profile of v3, /device:TPU:0, one launch (start us, length us, event | category | flops | bytes accessed | tf_op | source)
XLA Modules:
  0.0 45.9 jit_solution(2596709768106457531)
XLA Ops:
  0.0 44.0 %shard_map.82 = bf16[2,2,128,512]{3,2,1,0:T(8,128)(2,1)} custom-call(s32[16]{0:T(128)} %row_ref.1, s32[16]{0:T(128)} %col_ref.1, bf16[2,2,128,512]{3,2,1,0:T(8,128)(2,1)} %obj.1, bf16[2,128,128]{2,1,0:T(8,128)(2,1)} %probe.1, f32[128,128]{1,0:T(8,128)} %phase.1, f32[2,128,128]{2,1,0:T(8,128)} %measured.1, bf16[768,256]{1,0:T(8,128)(2,1)} %constant.4.clone.right, ...), custom_call_target="tpu_custom_call" | custom-call | tf_op jit(solution)/shard_map/pallas_call | solution.py:327
  44.0 1.9 %copy.10 = bf16[2,2,128,512]{3,2,1,0:T(8,128)(2,1)} copy(bf16[2,2,128,512]{3,2,1,0:T(8,128)(2,1)} %shard_map.82) | data formatting | bytes 1048576

commit v4 on v3

--- a/solution.py
+++ b/solution.py
@@ -21,9 +21,7 @@
     big = np.block([[real, imag], [-imag, real]]).astype(np.float32)
     high = big.astype(BF16)
     low = (big - high.astype(np.float32)).astype(BF16)
-    right = np.concatenate([high, high, low], axis=0)
-    left = np.concatenate([high.T, high.T, low.T], axis=1)
-    return right, left
+    return np.concatenate([high, high, low], axis=0)
 
 
 def split(value):
@@ -31,28 +29,17 @@
     return high, (value - high.astype(F32)).astype(BF16)
 
 
-def transform(field, right, left, window):
-    count = len(field)
-    high, low = split(
-        jnp.concatenate([jnp.concatenate([re, im], axis=1) for re, im in field], axis=0)
-    )
-    first = jnp.dot(
+def from_right(field, right, window):
+    high, low = split(jnp.concatenate(field, axis=1))
+    product = jnp.dot(
         jnp.concatenate([high, low, high], axis=1), right[...], preferred_element_type=F32
     )
-    rows = [first[p * window : (p + 1) * window] for p in range(count)]
-    high, low = split(
-        jnp.concatenate(
-            [jnp.concatenate([r[:, :window], r[:, window:]], axis=0) for r in rows], axis=1
-        )
-    )
-    second = jnp.dot(
-        left[...], jnp.concatenate([high, low, high], axis=0), preferred_element_type=F32
-    )
-    out = []
-    for p in range(count):
-        block = second[:, p * window : (p + 1) * window]
-        out.append((block[:window], block[window:]))
-    return out
+    return product[:, :window], product[:, window:]
+
+
+def transform(field, right, window):
+    first = [from_right(f, right, window) for f in field]
+    return [from_right((re.T, im.T), right, window) for re, im in first]
 
 
 def times(a, b):
@@ -94,9 +81,9 @@
 
 
 def kernel(
-    tiles, sections, row_ref, col_ref, obj, probe, phase, measured, right, left, out,
-    cut_prior, cut_own, low, patches, psi, work, terms, spill, spilled,
-    tile_send, tile_recv, cross_send, cross_recv, pair_send, pair_recv, back_send, back_recv,
+    tiles, sections, row_ref, col_ref, obj, probe, phase, measured, right_in, out,
+    cut_prior, cut_own, low, patches, psi, work, terms, spill, spilled, right, turned,
+    tile_send, tile_recv, cross_send, cross_recv, pair_send, pair_recv, back_send, back_recv, table_sem,
 ):
     layers, window, columns = obj.shape[1], obj.shape[2], obj.shape[3]
     count, slices = measured.shape[0], patches.shape[0]
@@ -115,6 +102,8 @@
             device_id=device, device_id_type=MESH,
         )
 
+    table = pltpu.make_async_copy(right_in, right, table_sem)
+    table.start()
     barrier = pltpu.get_barrier_semaphore()
     greeted = [{"tile": after}, {"tile": prior}, {"slab": partner}]
     for step in range(1, groups):
@@ -148,7 +137,10 @@
         tile_copy(layer).start()
     for layer in range(layers):
         cut(own_cols, layer, cut_own)
-    work[count] = jnp.concatenate([jnp.cos(phase[...]), jnp.sin(phase[...])], axis=1)
+    phase_turned = phase[...].T
+    work[count] = jnp.concatenate([jnp.cos(phase_turned), jnp.sin(phase_turned)], axis=1)
+    for p in range(count):
+        turned[p] = measured[p].T
 
     def cross_copy(step, layer):
         block = patches.at[first_own + layer]
@@ -212,7 +204,8 @@
         def _():
             pair_arrival(step, layer).wait_recv()
 
-    run = functools.partial(transform, right=right, left=left, window=window)
+    table.wait()
+    run = functools.partial(transform, right=right, window=window)
     start = (probe[0].astype(F32), probe[1].astype(F32))
     store(psi, 0, [start] * count)
 
@@ -244,7 +237,7 @@
     far = run(chi)
     shaped = []
     for p, (re, im) in enumerate(far):
-        misfit = re * re + im * im - measured[p]
+        misfit = re * re + im * im - turned[p]
         shaped.append((misfit * re, -(misfit * im)))
     grad = [conj(f) for f in run(shaped)]
     for p in range(count):
@@ -321,14 +314,15 @@
     tiles, sections = lax.axis_size("tile"), lax.axis_size("slab")
     slices = sections * layers
     groups = sections // 2
-    right, left = fourier_parts(window)
+    right = fourier_parts(window)
     wide = (layers, count, window, 2 * window)
     dma = pltpu.SemaphoreType.DMA
     return pl.pallas_call(
         functools.partial(kernel, tiles, sections),
         out_shape=jax.ShapeDtypeStruct(object_field.shape, BF16),
         in_specs=[pl.BlockSpec(memory_space=pltpu.SMEM)] * 2
-        + [pl.BlockSpec(memory_space=pltpu.VMEM)] * 6,
+        + [pl.BlockSpec(memory_space=pltpu.VMEM)] * 4
+        + [pl.BlockSpec(memory_space=pl.ANY)],
         out_specs=pl.BlockSpec(memory_space=pltpu.VMEM),
         scratch_shapes=[
             pltpu.VMEM(wide, BF16),
@@ -340,6 +334,8 @@
             pltpu.VMEM(wide, F32),
             pltpu.VMEM(wide, BF16),
             pltpu.VMEM(wide, BF16),
+            pltpu.VMEM(right.shape, BF16),
+            pltpu.VMEM(intensity.shape, F32),
             dma((layers,)),
             dma((layers,)),
             dma((groups - 1, layers)),
@@ -348,13 +344,14 @@
             dma((groups, layers)),
             dma((layers,)),
             dma((layers,)),
+            dma(()),
         ],
         compiler_params=pltpu.CompilerParams(
             collective_id=0, has_side_effects=True, vmem_limit_bytes=60 * 1024 * 1024
         ),
     )(
         patch_rows, patch_cols, object_field, probe_wave, prop_phase, intensity,
-        jnp.asarray(right), jnp.asarray(left),
+        jnp.asarray(right),
     )
 
 

time: 46.1 us -> 43.9 us (0.952)
  Pallas kernels: 44 us -> 41.8 us
    pallas_call x1, Pallas kernels: 44 us -> 41.8 us  [body(): pl.pallas_call(functools.partial(kernel, tiles, sections), out_shape=jax....]
where the time goes in v4:
time: 43.9 us; the launch traced here: 43.7 us
  Pallas kernels  41.8 us (95%)
  local copies, waits for them, and re-layouts  1.87 us (4%)
    pallas_call x1, Pallas kernels, body(): pl.pallas_call(functools.partial(kernel, tiles, sections), out_shape=jax....  41.8 us
    unnamed x1, local copies, waits for them, and re-layouts  1.87 us

profile of v4, /device:TPU:0, one launch (start us, length us, event | category | flops | bytes accessed | tf_op | source)
XLA Modules:
  0.0 43.7 jit_solution(11251584017198418153)
XLA Ops:
  0.0 41.8 %shard_map.73 = bf16[2,2,128,512]{3,2,1,0:T(8,128)(2,1)} custom-call(s32[16]{0:T(128)} %row_ref.1, s32[16]{0:T(128)} %col_ref.1, bf16[2,2,128,512]{3,2,1,0:T(8,128)(2,1)} %obj.1, bf16[2,128,128]{2,1,0:T(8,128)(2,1)} %probe.1, f32[128,128]{1,0:T(8,128)} %phase.1, f32[2,128,128]{2,1,0:T(8,128)} %measured.1, bf16[768,256]{1,0:T(8,128)(2,1)} %constant.2.clone.right_in), custom_call_target="tpu_custom_call" | custom-call | tf_op jit(solution)/shard_map/pallas_call | solution.py:320
  41.8 1.9 %copy.9 = bf16[2,2,128,512]{3,2,1,0:T(8,128)(2,1)} copy(bf16[2,2,128,512]{3,2,1,0:T(8,128)(2,1)} %shard_map.73) | data formatting | bytes 1048576

commit v5 on v4

--- a/solution.py
+++ b/solution.py
@@ -83,7 +83,7 @@
 def kernel(
     tiles, sections, row_ref, col_ref, obj, probe, phase, measured, right_in, out,
     cut_prior, cut_own, low, patches, psi, work, terms, spill, spilled, right, turned,
-    tile_send, tile_recv, cross_send, cross_recv, pair_send, pair_recv, back_send, back_recv, table_sem,
+    tile_send, tile_recv, cross_send, cross_recv, pair_send, pair_recv, back_send, back_recv, table_sem, go,
 ):
     layers, window, columns = obj.shape[1], obj.shape[2], obj.shape[3]
     count, slices = measured.shape[0], patches.shape[0]
@@ -133,14 +133,30 @@
     for layer in range(layers):
         cut(prior_cols, layer, cut_prior)
     pl.semaphore_wait(barrier, len(greeted))
-    for layer in range(layers):
-        tile_copy(layer).start()
+
+    @pl.when(side == 0)
+    def _():
+        for layer in range(layers):
+            tile_copy(layer).start()
+
     for layer in range(layers):
         cut(own_cols, layer, cut_own)
     phase_turned = phase[...].T
     work[count] = jnp.concatenate([jnp.cos(phase_turned), jnp.sin(phase_turned)], axis=1)
     for p in range(count):
         turned[p] = measured[p].T
+
+    @pl.when(side == 0)
+    def _():
+        for layer in range(layers):
+            tile_copy(layer).wait_send()
+        pl.semaphore_signal(go, inc=1, device_id={"slab": partner}, device_id_type=MESH)
+
+    @pl.when(side == 1)
+    def _():
+        pl.semaphore_wait(go, 1)
+        for layer in range(layers):
+            tile_copy(layer).start()
 
     def cross_copy(step, layer):
         block = patches.at[first_own + layer]
@@ -298,8 +314,13 @@
         total += jnp.dot(by_part(spilled, layer), prior_place, preferred_element_type=F32)
         out[0, layer] = total[:window].astype(out.dtype)
         out[1, layer] = total[window:].astype(out.dtype)
+
+    @pl.when(side == 1)
+    def _():
+        for layer in range(layers):
+            tile_copy(layer).wait_send()
+
     for layer in range(layers):
-        tile_copy(layer).wait_send()
         spill_copy(layer).wait_send()
         for step in range(1, groups):
             cross_copy(step, layer).wait_send()
@@ -319,7 +340,7 @@
     dma = pltpu.SemaphoreType.DMA
     return pl.pallas_call(
         functools.partial(kernel, tiles, sections),
-        out_shape=jax.ShapeDtypeStruct(object_field.shape, BF16),
+        out_shape=jax.ShapeDtypeStruct(object_field.shape, F32),
         in_specs=[pl.BlockSpec(memory_space=pltpu.SMEM)] * 2
         + [pl.BlockSpec(memory_space=pltpu.VMEM)] * 4
         + [pl.BlockSpec(memory_space=pl.ANY)],
@@ -345,6 +366,7 @@
             dma((layers,)),
             dma((layers,)),
             dma(()),
+            pltpu.SemaphoreType.REGULAR,
         ],
         compiler_params=pltpu.CompilerParams(
             collective_id=0, has_side_effects=True, vmem_limit_bytes=60 * 1024 * 1024
@@ -352,7 +374,7 @@
     )(
         patch_rows, patch_cols, object_field, probe_wave, prop_phase, intensity,
         jnp.asarray(right),
-    )
+    ).astype(BF16)
 
 
 def solution(mesh):

time: 43.9 us -> 43.9 us (level)
  other arithmetic: 0 us -> 2.08 us
  local copies, waits for them, and re-layouts: 1.87 us -> 0 us
    convert_element_type x0 -> x1, other arithmetic: none -> 2.08 us  [body(): return pl.pallas_call(functools.partial(kernel, tiles, sections), out_sha...]
    unnamed x1 -> x0, local copies, waits for them, and re-layouts: 1.87 us -> none
where the time goes in v5:
time: 43.9 us; the launch traced here: 43.7 us
  Pallas kernels  41.6 us (95%)
  other arithmetic  2.08 us (5%)
    pallas_call x1, Pallas kernels, body(): pl.pallas_call(functools.partial(kernel, tiles, sections), out_shape=jax....  41.6 us
    convert_element_type x1, other arithmetic, body(): return pl.pallas_call(functools.partial(kernel, tiles, sections), out_sha...  2.08 us

profile of v5, /device:TPU:0, one launch (start us, length us, event | category | flops | bytes accessed | tf_op | source)
XLA Modules:
  0.0 43.7 jit_solution(1325524641979050919)
XLA Ops:
  0.0 41.6 %shard_map.73 = f32[2,2,128,512]{3,2,1,0:T(8,128)} custom-call(s32[16]{0:T(128)} %row_ref.1, s32[16]{0:T(128)} %col_ref.1, bf16[2,2,128,512]{3,2,1,0:T(8,128)(2,1)} %obj.1, bf16[2,128,128]{2,1,0:T(8,128)(2,1)} %probe.1, f32[128,128]{1,0:T(8,128)} %phase.1, f32[2,128,128]{2,1,0:T(8,128)} %measured.1, bf16[768,256]{1,0:T(8,128)(2,1)} %constant.2.clone.right_in), custom_call_target="tpu_custom_call" | custom-call | tf_op jit(solution)/shard_map/pallas_call | solution.py:341
  41.6 2.1 %convert_element_type.3 = bf16[2,2,128,512]{3,2,1,0:T(8,128)(2,1)} convert(f32[2,2,128,512]{3,2,1,0:T(8,128)} %shard_map.73) | non-fusion elementwise | flops 262144 | bytes 1572864 | tf_op jit(solution)/shard_map/convert_element_type | solution.py:377

commit v6 on v5

--- a/solution.py
+++ b/solution.py
@@ -259,9 +259,10 @@
     for p in range(count):
         work[p] = jnp.concatenate(grad[p], axis=1)
 
-    def spill_copy(layer):
-        return remote(
-            spill.at[layer], spilled.at[layer], back_send.at[layer], back_recv.at[layer], tile=after
+    def spill_copy(layer, p):
+        return remote(
+            spill.at[layer, p], spilled.at[layer, p],
+            back_send.at[layer, p], back_recv.at[layer, p], tile=after,
         )
 
     def own_term(j):
@@ -280,7 +281,7 @@
                 )
                 terms[layer, p] = placed[:window]
                 spill[layer, p] = placed[window:].astype(BF16)
-            spill_copy(layer).start()
+                spill_copy(layer, p).start()
 
     def backward(i, carried):
         j = last - i
@@ -310,7 +311,8 @@
         high, low_part = split(by_part(terms, layer))
         total = jnp.dot(high, own_place, preferred_element_type=F32)
         total += jnp.dot(low_part, own_place, preferred_element_type=F32)
-        spill_copy(layer).wait_recv()
+        for p in range(count):
+            spill_copy(layer, p).wait_recv()
         total += jnp.dot(by_part(spilled, layer), prior_place, preferred_element_type=F32)
         out[0, layer] = total[:window].astype(out.dtype)
         out[1, layer] = total[window:].astype(out.dtype)
@@ -321,7 +323,8 @@
             tile_copy(layer).wait_send()
 
     for layer in range(layers):
-        spill_copy(layer).wait_send()
+        for p in range(count):
+            spill_copy(layer, p).wait_send()
         for step in range(1, groups):
             cross_copy(step, layer).wait_send()
         for step in range(groups):
@@ -340,7 +343,7 @@
     dma = pltpu.SemaphoreType.DMA
     return pl.pallas_call(
         functools.partial(kernel, tiles, sections),
-        out_shape=jax.ShapeDtypeStruct(object_field.shape, F32),
+        out_shape=jax.ShapeDtypeStruct(object_field.shape, BF16),
         in_specs=[pl.BlockSpec(memory_space=pltpu.SMEM)] * 2
         + [pl.BlockSpec(memory_space=pltpu.VMEM)] * 4
         + [pl.BlockSpec(memory_space=pl.ANY)],
@@ -363,8 +366,8 @@
             dma((groups - 1, layers)),
             dma((groups, layers)),
             dma((groups, layers)),
-            dma((layers,)),
-            dma((layers,)),
+            dma((layers, count)),
+            dma((layers, count)),
             dma(()),
             pltpu.SemaphoreType.REGULAR,
         ],
@@ -374,7 +377,7 @@
     )(
         patch_rows, patch_cols, object_field, probe_wave, prop_phase, intensity,
         jnp.asarray(right),
-    ).astype(BF16)
+    )
 
 
 def solution(mesh):

time: 43.9 us -> 43.6 us (level)
  other arithmetic: 2.08 us -> 0 us
  local copies, waits for them, and re-layouts: 0 us -> 1.87 us
    convert_element_type x1 -> x0, other arithmetic: 2.08 us -> none  [body(): return pl.pallas_call(functools.partial(kernel, tiles, sections), out_sha...]
    unnamed x0 -> x1, local copies, waits for them, and re-layouts: none -> 1.87 us
where the time goes in v6:
time: 43.6 us; the launch traced here: 43.5 us
  Pallas kernels  41.6 us (95%)
  local copies, waits for them, and re-layouts  1.87 us (4%)
    pallas_call x1, Pallas kernels, body(): pl.pallas_call(functools.partial(kernel, tiles, sections), out_shape=jax....  41.6 us
    unnamed x1, local copies, waits for them, and re-layouts  1.87 us

profile of v6, /device:TPU:0, one launch (start us, length us, event | category | flops | bytes accessed | tf_op | source)
XLA Modules:
  0.0 43.5 jit_solution(503068994888990903)
XLA Ops:
  0.0 41.6 %shard_map.73 = bf16[2,2,128,512]{3,2,1,0:T(8,128)(2,1)} custom-call(s32[16]{0:T(128)} %row_ref.1, s32[16]{0:T(128)} %col_ref.1, bf16[2,2,128,512]{3,2,1,0:T(8,128)(2,1)} %obj.1, bf16[2,128,128]{2,1,0:T(8,128)(2,1)} %probe.1, f32[128,128]{1,0:T(8,128)} %phase.1, f32[2,128,128]{2,1,0:T(8,128)} %measured.1, bf16[768,256]{1,0:T(8,128)(2,1)} %constant.2.clone.right_in), custom_call_target="tpu_custom_call" | custom-call | tf_op jit(solution)/shard_map/pallas_call | solution.py:344
  41.6 1.9 %copy.9 = bf16[2,2,128,512]{3,2,1,0:T(8,128)(2,1)} copy(bf16[2,2,128,512]{3,2,1,0:T(8,128)(2,1)} %shard_map.73) | data formatting | bytes 1048576

commit v7 on v6

--- a/solution.py
+++ b/solution.py
@@ -273,15 +273,16 @@
                 term = jnp.concatenate(
                     conj_times(halves(psi[j, p], window), halves(work[p], window)), axis=1
                 )
-                pick = one_hot((2 * window, window), 0, own_rows[p])
-                placed = jnp.dot(
-                    jnp.concatenate([pick, pick], axis=1),
-                    jnp.concatenate(split(term), axis=0),
-                    preferred_element_type=F32,
+                parts = jnp.concatenate(split(term), axis=0)
+                pick = one_hot((window, window), 0, own_rows[p] - window)
+                spill[layer, p] = jnp.dot(
+                    jnp.concatenate([pick, pick], axis=1), parts, preferred_element_type=F32
+                ).astype(BF16)
+                spill_copy(layer, p).start()
+                pick = one_hot((window, window), 0, own_rows[p])
+                terms[layer, p] = jnp.dot(
+                    jnp.concatenate([pick, pick], axis=1), parts, preferred_element_type=F32
                 )
-                terms[layer, p] = placed[:window]
-                spill[layer, p] = placed[window:].astype(BF16)
-                spill_copy(layer, p).start()
 
     def backward(i, carried):
         j = last - i

time: 43.6 us -> 43.6 us (level)
  no operation moved by 1% of the time
where the time goes in v7:
time: 43.6 us; the launch traced here: 43.4 us
  Pallas kernels  41.5 us (95%)
  local copies, waits for them, and re-layouts  1.87 us (4%)
    pallas_call x1, Pallas kernels, body(): pl.pallas_call(functools.partial(kernel, tiles, sections), out_shape=jax....  41.5 us
    unnamed x1, local copies, waits for them, and re-layouts  1.87 us

profile of v7, /device:TPU:0, one launch (start us, length us, event | category | flops | bytes accessed | tf_op | source)
XLA Modules:
  0.0 43.4 jit_solution(2649557367799685235)
XLA Ops:
  0.0 41.5 %shard_map.73 = bf16[2,2,128,512]{3,2,1,0:T(8,128)(2,1)} custom-call(s32[16]{0:T(128)} %row_ref.1, s32[16]{0:T(128)} %col_ref.1, bf16[2,2,128,512]{3,2,1,0:T(8,128)(2,1)} %obj.1, bf16[2,128,128]{2,1,0:T(8,128)(2,1)} %probe.1, f32[128,128]{1,0:T(8,128)} %phase.1, f32[2,128,128]{2,1,0:T(8,128)} %measured.1, bf16[768,256]{1,0:T(8,128)(2,1)} %constant.2.clone.right_in), custom_call_target="tpu_custom_call" | custom-call | tf_op jit(solution)/shard_map/pallas_call | solution.py:345
  41.5 1.9 %copy.9 = bf16[2,2,128,512]{3,2,1,0:T(8,128)(2,1)} copy(bf16[2,2,128,512]{3,2,1,0:T(8,128)(2,1)} %shard_map.73) | data formatting | bytes 1048576
